TPU v7x, 32 devices: a whole 2x2x4 slice. The times are simulated.
32 devices in a mesh: row: 8 (over y, x, core), col: 4 (over z).
Axes of the slice: x: 2, y: 2, z: 4, core: 2. Of those that a mesh axis runs over, the one named last changes fastest.
Arguments:
- matrix: float32 [8, 3, 256, 4, 6, 256], P('row', None, None, 'col'), as said below
- checksum: float32 [8, 3, 256, 6, 256], P('row'), as said below
- failed: int32 [4], P('col'), may hold values from 0 to 3, as said below
Outputs:
- factored: float32 [8, 3, 256, 4, 6, 256], P('row', None, None, 'col')
- updated_checksum_result: float32 [8, 3, 256, 6, 256], P('row')
Inputs may be any that keep to these rules, and one draw needn't show every extreme that they name: `failed`: a permutation of the grid column indices; entry 0 names the grid column whose tiles in matrix carry no information. With the lost grid column rebuilt from checksum, matrix is symmetric positive definite. `checksum`: for each grid row, the sum over all grid columns of the intact matrix's tiles, the lost column included.
All inputs are finite; a program needn't handle non-finite values.
Results may differ from a plain program's by a relative error of at most 0.0003.
Values sent between devices are 32-bit elements; how exact they have to be, the bound alone decides.
A program may use at most 128 MiB of HBM per device.

v0:
```python
import jax
import jax.numpy as jnp
from jax import lax
from jax.sharding import PartitionSpec as P

PANELS = 3


def spread_2(block, axis, holder):
    block = jnp.where(lax.axis_index(axis) == holder, block, jnp.zeros_like(block))
    return lax.psum(block, axis)


def solve_panel(column, factor, row_tiles, panel):
    tile_count, width = (column.shape[0], column.shape[1])
    stacked = column.reshape(tile_count * width, width)
    solved = jax.scipy.linalg.solve_triangular(factor, stacked.T, lower=True).T.reshape(
        tile_count, width, width
    )
    chosen = jnp.where((row_tiles > panel)[:, None, None], solved, 0.0)
    return jnp.where((row_tiles == panel)[:, None, None], factor[None, :, :], chosen)


def matching_tiles(panel_rows, column_position, rows_count, cols_count):
    width = panel_rows.shape[1]
    repeats = max(rows_count // cols_count, 1)
    received = []
    for offset in range(repeats):
        source = (column_position + offset * cols_count) % rows_count
        received.append(spread_2(panel_rows, "row", source))
    return jnp.stack(received, axis=1).reshape(-1, width, width)


def shards(matrix, checksum, failed):
    rows_count = lax.axis_size("row")
    cols_count = lax.axis_size("col")
    row_index = lax.axis_index("row")
    column_position = lax.axis_index("col")
    tile_rows, width, tile_cols = (matrix.shape[1], matrix.shape[2], matrix.shape[4])
    resident_tiles = matrix.reshape(tile_rows, width, tile_cols, width)
    totals = checksum.reshape(tile_rows, width, tile_cols, width)
    missing_tiles = lax.all_gather(failed, "col", axis=0, tiled=True)[0]
    healthy_member = jnp.where(column_position != missing_tiles, resident_tiles, 0.0)
    remaining_peers = lax.psum(healthy_member, "col")
    work = jnp.where(column_position == missing_tiles, totals - remaining_peers, resident_tiles)
    row_tiles = row_index + jnp.arange(tile_rows, dtype=jnp.int32) * rows_count
    col_tiles = column_position + jnp.arange(tile_cols, dtype=jnp.int32) * cols_count
    identity = jnp.eye(width, dtype=jnp.float32)
    finished = []
    for panel in range(PANELS):
        col_root = panel % cols_count
        col_slot = panel // cols_count
        row_root = panel % rows_count
        row_slot = panel // rows_count
        column = work[:, :, col_slot, :]
        owner = jnp.logical_and(row_index == row_root, column_position == col_root)
        diag_input = jnp.where(owner, work[row_slot, :, col_slot, :], identity)
        factor_here = jnp.linalg.cholesky(diag_input)
        factor = spread_2(factor_here, "row", row_root)
        own_rows = solve_panel(column, factor, row_tiles, panel)
        panel_rows = spread_2(own_rows, "col", col_root)
        panel_cols = matching_tiles(panel_rows, column_position, rows_count, cols_count)
        update = jnp.einsum(
            "axr,byr->axby", panel_rows, panel_cols, precision=lax.Precision.HIGHEST
        )
        work = work - update
        finished.append((col_root, col_slot, panel_rows))
    totals = lax.psum(work, "col")
    for col_root, col_slot, panel_rows in finished:
        current = work[:, :, col_slot, :]
        work = work.at[:, :, col_slot, :].set(
            jnp.where(column_position == col_root, panel_rows, current)
        )
    keep = (row_tiles[:, None] >= col_tiles[None, :])[:, None, :, None]
    factored = jnp.where(keep, work, 0.0).reshape(matrix.shape)
    return (factored, totals.reshape(checksum.shape))


def solution(mesh):
    return jax.shard_map(
        shards,
        mesh=mesh,
        in_specs=(
            P("row", None, None, "col", None, None),
            P("row", None, None, None, None),
            P("col"),
        ),
        out_specs=(P("row", None, None, "col", None, None), P("row", None, None, None, None)),
        check_vma=False,
    )
```

profile of v0, /device:TPU:0, one launch (start us, length us, event | category | flops | bytes accessed | tf_op | source)
XLA Modules:
  0.0 1121.8 jit_solution(12888516157622875369)
XLA Ops:
  7.9 1.2 dynamic-slice.31
  9.9 9.9 all-reduce.1
  19.8 12.1 %copy.25 = f32[1,3,256,1,6,256]{2,5,4,1,3,0:T(8,128)} copy(f32[1,3,256,1,6,256]{5,3,4,2,1,0:T(1,128)} %param.12) | data formatting | bytes 9437184 | tf_op args[0]
  31.9 5.0 bitcast_select_fusion.1
  37.0 6.1 copy.24
  43.1 165.1 %all-reduce.17.cloned.1.call-done = f32[3,256,6,256]{1,3,2,0:T(8,128)} async-done(((f32[3,256,6,256]{1,3,2,0:T(8,128)}), f32[3,256,6,256]{1,3,2,0:T(8,128)}) %all-reduce.17.cloned.1.call-update) | async-done | bytes 4718608 | tf_op jit(solution)/shard_map/psum | solution.py:44
  208.2 6.3 bitcast_select_fusion
  214.5 2.2 copy-done.1
  216.9 1.1 fusion.12
  217.9 11.7 %cholesky.172 = f32[128,128]{1,0:T(8,128)S(1)} custom-call(f32[128,128]{1,0:T(8,128)S(1)} %cholesky.270), custom_call_target="Cholesky" | custom-call | tf_op jit(solution)/shard_map/jit(cholesky)/cholesky | solution.py:58
  229.7 9.8 custom-call.15
  240.0 11.7 %cholesky.189 = f32[128,128]{1,0:T(8,128)S(1)} custom-call(f32[128,128]{1,0:T(8,128)S(1)} %convolution_subtract_fusion.8), custom_call_target="Cholesky" | custom-call | tf_op jit(solution)/shard_map/jit(cholesky)/cholesky | solution.py:58
  255.1 52.3 %all-reduce.19.cloned.1.call-done = f32[256,256]{1,0:T(8,128)} async-done(((f32[256,256]{1,0:T(8,128)}), f32[256,256]{1,0:T(8,128)}) %all-reduce.19.cloned.1.call-update) | async-done | bytes 262160 | tf_op jit(solution)/shard_map/psum | solution.py:11
  308.5 4.0 while.9
  309.1 1.4 bitcast_dynamic-update-slice_fusion.9
  311.1 1.4 bitcast_dynamic-update-slice_fusion.9
  312.5 19.7 %custom-call.16 = f32[2,128,128]{1,2,0:T(8,128)S(1)} custom-call(f32[2,128,128]{2,1,0:T(8,128)S(1)} %get-tuple-element.60), custom_call_target="InvertDiagBlocksLowerTriangular" | custom-call | tf_op jit(solution)/shard_map/jit(_solve_triangular)/triangular_solve | solution.py:17
  334.8 1.0 select_select_fusion.2
  335.9 43.3 %all-reduce.21.cloned.1.call-done = f32[3,256,256]{1,2,0:T(8,128)} async-done(((f32[3,256,256]{1,2,0:T(8,128)}), f32[3,256,256]{1,2,0:T(8,128)}) %all-reduce.21.cloned.1.call-update) | async-done | bytes 786448 | tf_op jit(solution)/shard_map/psum | solution.py:11
  379.3 2.5 select_bitcast_fusion.6
  381.8 59.4 %all-reduce.37.cloned.1.call-done = (f32[3,1,256,256]{2,3,0,1:T(8,128)}, f32[3,1,256,256]{2,3,0,1:T(8,128)}) async-done(((f32[3,1,256,256]{2,3,0,1:T(8,128)}, f32[3,1,256,256]{2,3,0,1:T(8,128)}), (f32[3,1,256,256]{2,3,0,1:T(8,128)}, f32[3,1,256,256]{2,3,0,1:T(8,128)})) %all-reduce.37.cloned.1.call-update) | async-done | bytes 1572880 | tf_op jit(solution)/shard_map/psum | solution.py:11
  441.2 1.5 pad_maximum_fusion
  442.7 1.6 copy.31
  444.3 7.3 convolution_subtract_fusion.2
  451.7 2.2 copy-done.2
  454.0 1.1 fusion.11
  455.1 11.7 %cholesky.206 = f32[128,128]{1,0:T(8,128)S(1)} custom-call(f32[128,128]{1,0:T(8,128)S(1)} %cholesky.273), custom_call_target="Cholesky" | custom-call | tf_op jit(solution)/shard_map/jit(cholesky)/cholesky | solution.py:58
  467.5 9.8 custom-call.17
  477.8 11.9 %cholesky.223 = f32[128,128]{1,0:T(8,128)S(1)} custom-call(f32[128,128]{1,0:T(8,128)S(1)} %convolution_subtract_fusion.7), custom_call_target="Cholesky" | custom-call | tf_op jit(solution)/shard_map/jit(cholesky)/cholesky | solution.py:58
  492.7 52.9 %all-reduce.23.cloned.1.call-done = f32[256,256]{1,0:T(8,128)} async-done(((f32[256,256]{1,0:T(8,128)}), f32[256,256]{1,0:T(8,128)}) %all-reduce.23.cloned.1.call-update) | async-done | bytes 262160 | tf_op jit(solution)/shard_map/psum | solution.py:11
  546.6 4.0 while.10
  547.2 1.4 bitcast_dynamic-update-slice_fusion.10
  549.2 1.4 bitcast_dynamic-update-slice_fusion.10
  550.6 19.7 %custom-call.18 = f32[2,128,128]{1,2,0:T(8,128)S(1)} custom-call(f32[2,128,128]{2,1,0:T(8,128)S(1)} %get-tuple-element.61), custom_call_target="InvertDiagBlocksLowerTriangular" | custom-call | tf_op jit(solution)/shard_map/jit(_solve_triangular)/triangular_solve | solution.py:17
  572.9 1.0 select_select_fusion.1
  574.0 43.4 %all-reduce.25.cloned.1.call-done = f32[3,256,256]{1,2,0:T(8,128)} async-done(((f32[3,256,256]{1,2,0:T(8,128)}), f32[3,256,256]{1,2,0:T(8,128)}) %all-reduce.25.cloned.1.call-update) | async-done | bytes 786448 | tf_op jit(solution)/shard_map/psum | solution.py:11
  617.4 2.5 select_bitcast_fusion.4
  620.2 59.3 %all-reduce.35.cloned.1.call-done = (f32[3,1,256,256]{2,3,0,1:T(8,128)}, f32[3,1,256,256]{2,3,0,1:T(8,128)}) async-done(((f32[3,1,256,256]{2,3,0,1:T(8,128)}, f32[3,1,256,256]{2,3,0,1:T(8,128)}), (f32[3,1,256,256]{2,3,0,1:T(8,128)}, f32[3,1,256,256]{2,3,0,1:T(8,128)})) %all-reduce.35.cloned.1.call-update) | async-done | bytes 1572880 | tf_op jit(solution)/shard_map/psum | solution.py:11
  679.5 2.7 pad_maximum_fusion.1
  682.2 3.0 copy.39
  685.2 7.3 convolution_subtract_fusion.1
  692.6 2.2 copy-done.3
  694.9 1.1 fusion.10
  696.0 11.7 %cholesky.240 = f32[128,128]{1,0:T(8,128)S(1)} custom-call(f32[128,128]{1,0:T(8,128)S(1)} %cholesky.276), custom_call_target="Cholesky" | custom-call | tf_op jit(solution)/shard_map/jit(cholesky)/cholesky | solution.py:58
  708.4 9.8 custom-call.19
  718.7 11.9 %cholesky.257 = f32[128,128]{1,0:T(8,128)S(1)} custom-call(f32[128,128]{1,0:T(8,128)S(1)} %convolution_subtract_fusion.6), custom_call_target="Cholesky" | custom-call | tf_op jit(solution)/shard_map/jit(cholesky)/cholesky | solution.py:58
  733.7 52.9 %all-reduce.27.cloned.1.call-done = f32[256,256]{1,0:T(8,128)} async-done(((f32[256,256]{1,0:T(8,128)}), f32[256,256]{1,0:T(8,128)}) %all-reduce.27.cloned.1.call-update) | async-done | bytes 262160 | tf_op jit(solution)/shard_map/psum | solution.py:11
  787.6 4.0 while.11
  788.3 1.4 bitcast_dynamic-update-slice_fusion.11
  790.2 1.4 bitcast_dynamic-update-slice_fusion.11
  791.6 19.7 %custom-call.20 = f32[2,128,128]{1,2,0:T(8,128)S(1)} custom-call(f32[2,128,128]{2,1,0:T(8,128)S(1)} %get-tuple-element.62), custom_call_target="InvertDiagBlocksLowerTriangular" | custom-call | tf_op jit(solution)/shard_map/jit(_solve_triangular)/triangular_solve | solution.py:17
  815.0 43.4 %all-reduce.29.cloned.1.call-done = f32[3,256,256]{1,2,0:T(8,128)} async-done(((f32[3,256,256]{1,2,0:T(8,128)}), f32[3,256,256]{1,2,0:T(8,128)}) %all-reduce.29.cloned.1.call-update) | async-done | bytes 786448 | tf_op jit(solution)/shard_map/psum | solution.py:11
  858.4 2.5 select_bitcast_fusion.2
  861.3 59.1 %all-reduce.33.cloned.1.call-done = (f32[3,1,256,256]{2,3,0,1:T(8,128)}, f32[3,1,256,256]{2,3,0,1:T(8,128)}) async-done(((f32[3,1,256,256]{2,3,0,1:T(8,128)}, f32[3,1,256,256]{2,3,0,1:T(8,128)}), (f32[3,1,256,256]{2,3,0,1:T(8,128)}, f32[3,1,256,256]{2,3,0,1:T(8,128)})) %all-reduce.33.cloned.1.call-update) | async-done | bytes 1572880 | tf_op jit(solution)/shard_map/psum | solution.py:11
  920.4 2.7 pad_maximum_fusion.2
  923.1 3.0 copy.47
  926.1 7.0 convolution_subtract_fusion
  933.1 2.2 copy-done
  935.2 2.2 copy.112
  937.5 1.2 fusion
  941.7 5.7 select_bitcast_fusion
  947.4 12.1 %copy.53 = f32[1,3,256,1,6,256]{5,3,4,2,1,0:T(1,128)} copy(f32[1,3,256,1,6,256]{2,5,4,1,3,0:T(8,128)} %select_bitcast_fusion) | data formatting | bytes 9437184
  959.5 149.2 %all-reduce.31.cloned.1.call-done = f32[1,3,256,6,256]{2,4,3,1,0:T(8,128)} async-done(((f32[1,3,256,6,256]{2,4,3,1,0:T(8,128)}), f32[1,3,256,6,256]{2,4,3,1,0:T(8,128)}) %all-reduce.31.cloned.1.call-update) | async-done | bytes 4718608 | tf_op jit(solution)/shard_map/psum | solution.py:68
  1108.7 6.0 copy.54
  (132 shorter events, 29.1 us)
Async XLA Ops:
  7.2 201.1 %all-reduce.17.cloned.1.call-start = ((), (), s32[]{:S(2)}) async-start(), calls=%async_computation | async-start | bytes 9437184 | tf_op jit(solution)/shard_map/psum | solution.py:44
  36.9 270.5 %all-reduce.19.cloned.1.call-start = ((), (), s32[]{:S(2)}) async-start(), calls=%async_computation.1 | async-start | bytes 524288 | tf_op jit(solution)/shard_map/psum | solution.py:11
  214.5 2.2 copy-start.1
  216.7 38.1 %slice-start = ((f32[3,256,6,256]{1,3,2,0:T(8,128)}), f32[3,256,1,256]{1,3,2,0:T(8,128)S(1)}, s32[]{:S(2)}) async-start(f32[3,256,6,256]{1,3,2,0:T(8,128)} %copy-done.1), calls=%async_computation.11 | async-start | bytes 1572864 | tf_op jit(solution)/shard_map/slice | solution.py:55
  254.4 124.9 %all-reduce.21.cloned.1.call-start = ((), (), s32[]{:S(2)}) async-start(), calls=%async_computation.2 | async-start | bytes 1572864 | tf_op jit(solution)/shard_map/psum | solution.py:11
  307.4 27.3 %copy-start.7 = (f32[256,256]{1,0:T(8,128)S(1)}, f32[256,256]{1,0:T(8,128)}, u32[]{:S(2)}) copy-start(f32[256,256]{1,0:T(8,128)} %all-reduce.19.cloned.1.call-done) | copy-start | bytes 786436
  335.8 105.4 %all-reduce.37.cloned.1.call-start = ((), (), s32[]{:S(2)}) async-start(), calls=%async_computation.10 | async-start | bytes 3145728 | tf_op jit(solution)/shard_map/psum | solution.py:11
  379.3 65.0 %copy-start.5 = (f32[3,256,256]{1,2,0:T(8,128)S(1)}, f32[3,256,256]{1,2,0:T(8,128)}, u32[]{:S(2)}) copy-start(f32[3,256,256]{1,2,0:T(8,128)} %all-reduce.21.cloned.1.call-done) | copy-start | bytes 2359300
  381.8 163.8 %all-reduce.23.cloned.1.call-start = ((), (), s32[]{:S(2)}) async-start(), calls=%async_computation.3 | async-start | bytes 524288 | tf_op jit(solution)/shard_map/psum | solution.py:11
  451.7 2.2 copy-start.2
  453.9 38.5 %slice-start.1 = ((f32[3,256,6,256]{1,3,2,0:T(8,128)}), f32[3,256,1,256]{1,3,2,0:T(8,128)S(1)}, s32[]{:S(2)}) async-start(f32[3,256,6,256]{1,3,2,0:T(8,128)} %copy-done.2), calls=%async_computation.12 | async-start | bytes 1572864 | tf_op jit(solution)/shard_map/slice | solution.py:55
  492.3 125.1 %all-reduce.25.cloned.1.call-start = ((), (), s32[]{:S(2)}) async-start(), calls=%async_computation.4 | async-start | bytes 1572864 | tf_op jit(solution)/shard_map/psum | solution.py:11
  545.6 27.2 %copy-start.9 = (f32[256,256]{1,0:T(8,128)S(1)}, f32[256,256]{1,0:T(8,128)}, u32[]{:S(2)}) copy-start(f32[256,256]{1,0:T(8,128)} %all-reduce.23.cloned.1.call-done) | copy-start | bytes 786436
  574.0 105.5 %all-reduce.35.cloned.1.call-start = ((), (), s32[]{:S(2)}) async-start(), calls=%async_computation.9 | async-start | bytes 3145728 | tf_op jit(solution)/shard_map/psum | solution.py:11
  617.4 67.8 %copy-start.4 = (f32[3,256,256]{1,2,0:T(8,128)S(1)}, f32[3,256,256]{1,2,0:T(8,128)}, u32[]{:S(2)}) copy-start(f32[3,256,256]{1,2,0:T(8,128)} %all-reduce.25.cloned.1.call-done) | copy-start | bytes 2359300
  619.9 166.7 %all-reduce.27.cloned.1.call-start = ((), (), s32[]{:S(2)}) async-start(), calls=%async_computation.5 | async-start | bytes 524288 | tf_op jit(solution)/shard_map/psum | solution.py:11
  692.6 2.2 copy-start.3
  694.8 38.6 %slice-start.2 = ((f32[3,256,6,256]{1,3,2,0:T(8,128)}), f32[3,256,1,256]{1,3,2,0:T(8,128)S(1)}, s32[]{:S(2)}) async-start(f32[3,256,6,256]{1,3,2,0:T(8,128)} %copy-done.3), calls=%async_computation.13 | async-start | bytes 1572864 | tf_op jit(solution)/shard_map/slice | solution.py:55
  733.3 125.1 %all-reduce.29.cloned.1.call-start = ((), (), s32[]{:S(2)}) async-start(), calls=%async_computation.6 | async-start | bytes 1572864 | tf_op jit(solution)/shard_map/psum | solution.py:11
  786.6 27.2 %copy-start.8 = (f32[256,256]{1,0:T(8,128)S(1)}, f32[256,256]{1,0:T(8,128)}, u32[]{:S(2)}) copy-start(f32[256,256]{1,0:T(8,128)} %all-reduce.27.cloned.1.call-done) | copy-start | bytes 786436
  815.0 105.4 %all-reduce.33.cloned.1.call-start = ((), (), s32[]{:S(2)}) async-start(), calls=%async_computation.8 | async-start | bytes 3145728 | tf_op jit(solution)/shard_map/psum | solution.py:11
  858.4 67.7 %copy-start.6 = (f32[3,256,256]{1,2,0:T(8,128)S(1)}, f32[3,256,256]{1,2,0:T(8,128)}, u32[]{:S(2)}) copy-start(f32[3,256,256]{1,2,0:T(8,128)} %all-reduce.29.cloned.1.call-done) | copy-start | bytes 2359300
  860.9 247.8 %all-reduce.31.cloned.1.call-start = ((), (), s32[]{:S(2)}) async-start(), calls=%async_computation.7 | async-start | bytes 9437184 | tf_op jit(solution)/shard_map/psum | solution.py:68
  933.1 2.2 copy-start
Sparse Core Ops, SparseCore 0:
  37.0 171.1 all-reduce.16
  254.5 52.8 all-reduce.18
  336.0 43.2 all-reduce.20
  383.0 58.2 all-reduce.36
  492.4 53.0 all-reduce.22
  574.1 43.2 all-reduce.24
  621.2 58.2 all-reduce.34
  733.4 53.0 all-reduce.26
  815.1 43.2 all-reduce.28
  862.1 58.2 all-reduce.32
  937.6 171.1 all-reduce.30
where the time goes:
time: 1130 us; the launch traced here: 1120 us
  waiting for transfers between devices  780 us (69%)
  other arithmetic  209 us (18%)
  local copies, waits for them, and re-layouts  72.9 us (6%)
  matrix products  28.6 us (3%)
  between operations  19.4 us (2%)
    psum x9, waiting for transfers between devices, spread_2(): return lax.psum(block, axis)  466 us
    psum x1, waiting for transfers between devices, shards(): remaining_peers = lax.psum(healthy_member, 'col')  165 us
    psum x1, waiting for transfers between devices, shards(): totals = lax.psum(work, 'col')  149 us
    another operation x20, other arithmetic, shards(): factor_here = jnp.linalg.cholesky(diag_input)  103 us
    another operation x7, other arithmetic, solve_panel(): jax.scipy.linalg.solve_triangular(factor, stacked.T, lower=True)  62.1 us
    unnamed x28, local copies, waits for them, and re-layouts  49.2 us
  transfers between devices with their start and end apart: 11, of which 11 were waited for; matrix products, arithmetic and copies ran while one was open for 3% of the time, Pallas kernels for 0%

commit v1 on v0

v1 whole, which is shorter than its diff:
```python
import jax
import jax.numpy as jnp
from jax import lax
from jax.sharding import PartitionSpec as P

PANELS = 3
EXACT = lax.Precision.HIGHEST
FAST = lax.Precision.HIGH


def dot_t(a, b, precision=EXACT):
    return lax.dot_general(a, b, (((1,), (1,)), ((), ())), precision=precision)


def dot(a, b, precision=EXACT):
    return lax.dot_general(a, b, (((1,), (0,)), ((), ())), precision=precision)


def shards(matrix, checksum, failed):
    rows_count = lax.axis_size("row")
    cols_count = lax.axis_size("col")
    row_index = lax.axis_index("row")
    column_position = lax.axis_index("col")
    tile_rows, width, tile_cols = (matrix.shape[1], matrix.shape[2], matrix.shape[4])
    own = matrix.reshape(tile_rows, width, tile_cols, width).transpose(0, 2, 1, 3)
    totals = checksum.reshape(tile_rows, width, tile_cols, width).transpose(0, 2, 1, 3)
    row_tiles = row_index + jnp.arange(tile_rows, dtype=jnp.int32) * rows_count
    col_tiles = column_position + jnp.arange(tile_cols, dtype=jnp.int32) * cols_count
    slots = (PANELS - 1) // cols_count + 1
    top_slots = (PANELS - 1) // rows_count + 1

    lost_column = lax.all_gather(failed, "col", axis=0, tiled=True)[0]
    lost = column_position == lost_column

    gathered = lax.all_gather(own[:, :slots], "col", axis=0)
    ids = jnp.arange(cols_count, dtype=jnp.int32).reshape(-1, 1, 1, 1, 1)
    others = jnp.sum(jnp.where(ids != lost_column, gathered, 0.0), axis=0)
    patch = totals[:, :slots] - others
    panels = []
    for k in range(PANELS):
        slot = k // cols_count
        panels.append(
            jnp.where(lost_column == k % cols_count, patch[:, slot], gathered[k % cols_count, :, slot])
        )

    lead = jnp.stack(
        [
            jnp.where(
                row_index == i % rows_count,
                jnp.stack([panels[k][i // rows_count] for k in range(i + 1)] + [
                    jnp.zeros((width, width), jnp.float32) for _ in range(i + 1, PANELS)
                ]),
                0.0,
            )
            for i in range(PANELS)
        ]
    )
    lead = lax.psum(lead, "row")

    need = [
        tile_cols
        if a < top_slots
        else min(tile_cols, (rows_count * (a + 1) - 1) // cols_count + 1)
        for a in range(tile_rows)
    ]
    packed = jnp.concatenate([own[a, : need[a]] for a in range(tile_rows)], axis=0)
    lead_done, packed = lax.optimization_barrier((lead, packed))
    lead = lead_done
    summed = lax.psum(jnp.where(lost, 0.0, packed), "col")
    filled = []
    start = 0
    for a in range(tile_rows):
        pad = jnp.zeros((tile_cols - need[a], width, width), jnp.float32)
        filled.append(jnp.concatenate([summed[start : start + need[a]], pad], axis=0))
        start += need[a]
    work = jnp.where(lost, totals - jnp.stack(filled), own)

    tops = jnp.stack(
        [
            jnp.where(
                row_index == i % rows_count,
                jnp.concatenate([work[i // rows_count], totals[i // rows_count]], axis=0),
                0.0,
            )
            for i in range(PANELS)
        ]
    )
    tops = lax.psum(tops, "row")

    identity = jnp.eye(width, dtype=jnp.float32)
    factor = {}
    inverse = []
    for k in range(PANELS):
        for i in range(k, PANELS):
            tile = lead[i, k]
            for m in range(k):
                tile = tile - dot_t(factor[i, m], factor[k, m])
            if i == k:
                factor[k, k] = jnp.linalg.cholesky(tile)
                inverse.append(
                    jax.scipy.linalg.solve_triangular(factor[k, k], identity, lower=True)
                )
            else:
                factor[i, k] = dot_t(tile, inverse[k])

    solved_rows = []
    for k in range(PANELS):
        block = panels[k].reshape(tile_rows * width, width)
        for m in range(k):
            block = block - dot_t(solved_rows[m], factor[k, m])
        block = dot_t(block, inverse[k]).reshape(tile_rows, width, width)
        block = jnp.where((row_tiles > k)[:, None, None], block, 0.0)
        block = jnp.where((row_tiles == k)[:, None, None], factor[k, k][None], block)
        solved_rows.append(block.reshape(tile_rows * width, width))

    flat = tops.transpose(0, 2, 1, 3).reshape(PANELS, width, 2 * tile_cols * width)
    solved_cols = []
    for k in range(PANELS):
        block = flat[k]
        for m in range(k):
            block = block - dot(factor[k, m], solved_cols[m])
        solved_cols.append(dot(inverse[k], block))

    rows_factor = jnp.concatenate(solved_rows, axis=1)
    cols_factor = jnp.concatenate(solved_cols, axis=0)
    split = tile_cols * width
    shape = (tile_rows, width, tile_cols, width)
    update = dot(rows_factor, cols_factor[:, :split], FAST).reshape(shape).transpose(0, 2, 1, 3)
    drop = dot(rows_factor, cols_factor[:, split:], FAST).reshape(shape).transpose(0, 2, 1, 3)
    new_totals = (totals - drop).transpose(0, 2, 1, 3)

    work = work - update
    front = []
    for b in range(slots):
        tiles = work[:, b]
        for k in range(PANELS):
            if k // cols_count == b:
                mine = solved_rows[k].reshape(tile_rows, width, width)
                tiles = jnp.where(column_position == k % cols_count, mine, tiles)
        front.append(tiles)
    work = jnp.concatenate([jnp.stack(front, axis=1), work[:, slots:]], axis=1)
    keep = (row_tiles[:, None] >= col_tiles[None, :])[:, :, None, None]
    factored = jnp.where(keep, work, 0.0).transpose(0, 2, 1, 3)
    return (factored.reshape(matrix.shape), new_totals.reshape(checksum.shape))


def solution(mesh):
    return jax.shard_map(
        shards,
        mesh=mesh,
        in_specs=(
            P("row", None, None, "col", None, None),
            P("row", None, None, None, None),
            P("col"),
        ),
        out_specs=(P("row", None, None, "col", None, None), P("row", None, None, None, None)),
        check_vma=False,
    )
```

time: 1130 us -> 607 us (0.54)
  waiting for transfers between devices: 780 us -> 168 us
  local copies, waits for them, and re-layouts: 72.9 us -> 122 us
  matrix products: 28.6 us -> 65.9 us
    psum x11 -> x3, waiting for transfers between devices: 780 us -> 125 us  [the longest x1 52.6 us: shards(): lead = lax.psum(lead, 'row')]
    all_gather x0 -> x1, waiting for transfers between devices: none -> 43.6 us  [shards(): gathered = lax.all_gather(own[:, :slots], 'col', axis=0)]
    dot_general x3 -> x21, matrix products: 21.6 us -> 58.6 us  [the longest x8 41.3 us: dot(): return lax.dot_general(a, b, (((1,), (0,)), ((), ())), precision=precision)]
    reshape x3 -> x5, local copies, waits for them, and re-layouts: 0.79 us -> 23.7 us  [the longest x2 12.9 us: shards(): dot(rows_factor, cols_factor[:, :split], FAST).reshape(shape)]
    slice x9 -> x11, local copies, waits for them, and re-layouts: 0.81 us -> 17.9 us  [the longest x1 7.46 us: shards(): block = flat[k]]
    another operation x33 -> x29, other arithmetic: 180 us -> 168 us  [the longest x20 104 us: shards(): factor[k, k] = jnp.linalg.cholesky(tile)]
    sub x0 -> x2, other arithmetic: none -> 11.6 us  [the longest x1 7.17 us: shards(): new_totals = (totals - drop).transpose(0, 2, 1, 3)]
    unnamed x28 -> x124, local copies, waits for them, and re-layouts: 49.2 us -> 46.6 us
  transfers between devices with their start and end apart: 11 -> 4, of which waited for: 11 -> 4; matrix products, arithmetic and copies ran while one was open for 3% -> 39% of each run, Pallas kernels for 0% -> 0%
where the time goes in v1:
time: 607 us; the launch traced here: 600 us
  other arithmetic  213 us (35%)
  waiting for transfers between devices  168 us (28%)
  local copies, waits for them, and re-layouts  122 us (20%)
  matrix products  65.9 us (11%)
  between operations  19.8 us (3%)
  blocking collectives  9.92 us (2%)
    another operation x20, other arithmetic, shards(): factor[k, k] = jnp.linalg.cholesky(tile)  104 us
    another operation x7, other arithmetic, shards(): jax.scipy.linalg.solve_triangular(factor[k, k], identity, lower=True)  62.5 us
    psum x1, waiting for transfers between devices, shards(): lead = lax.psum(lead, 'row')  52.6 us
    psum x1, waiting for transfers between devices, shards(): tops = lax.psum(tops, 'row')  51.3 us
    unnamed x124, local copies, waits for them, and re-layouts  46.6 us
    all_gather x1, waiting for transfers between devices, shards(): gathered = lax.all_gather(own[:, :slots], 'col', axis=0)  43.6 us
    dot_general x8, matrix products, dot(): return lax.dot_general(a, b, (((1,), (0,)), ((), ())), precision=precision)  41.3 us
    psum x1, waiting for transfers between devices, shards(): summed = lax.psum(jnp.where(lost, 0.0, packed), 'col')  20.6 us
  transfers between devices with their start and end apart: 4, of which 4 were waited for; matrix products, arithmetic and copies ran while one was open for 39% of the time, Pallas kernels for 0%

profile of v1, /device:TPU:0, one launch (start us, length us, event | category | flops | bytes accessed | tf_op | source)
XLA Modules:
  0.0 600.1 jit_solution(15367717784824096456)
XLA Ops:
  7.2 12.1 %copy.79 = f32[1,3,256,1,6,256]{2,5,4,1,3,0:T(8,128)} copy(f32[1,3,256,1,6,256]{5,3,4,2,1,0:T(1,128)} %param.6) | data formatting | bytes 9437184 | tf_op args[0]
  23.7 9.9 %all-reduce.2 = s32[4]{0:T(128)S(1)} all-reduce(s32[4]{0:T(128)S(1)} %dynamic-update-slice.10), channel_id=1, replica_groups=mesh['row'=8,'col'=4] {'col'}, use_global_device_ids=true, to_apply=%add.2 | all-reduce | flops 4 | bytes 32
  33.8 6.1 %copy.78 = f32[1,3,256,6,256]{2,4,3,1,0:T(8,128)} copy(f32[1,3,256,6,256]{4,2,3,1,0:T(8,128)} %param.7) | data formatting | bytes 9437184 | tf_op args[1]
  39.9 2.7 slice.200
  44.4 43.6 %all-gather.3.cloned.1.call-done = f32[12,1,256,256]{3,2,1,0:T(8,128)} async-done(((f32[3,1,256,256]{3,2,1,0:T(8,128)}), f32[12,1,256,256]{3,2,1,0:T(8,128)}) %all-gather.3.cloned.1.call-update) | async-done | bytes 3145744 | tf_op jit(solution)/shard_map/all_gather | solution.py:35
  88.0 3.3 fusion.84
  91.3 2.3 copy.118
  96.2 2.4 copy.119
  98.5 1.8 broadcast_select_fusion.2
  101.6 1.6 fusion.15
  103.3 1.6 pad_maximum_fusion.3
  106.4 2.3 slice_bitcast_fusion.3
  108.7 2.5 pad_maximum_fusion.1
  114.0 52.6 %all-reduce.7.cloned.1.call-done = f32[3,3,256,256]{2,3,1,0:T(8,128)} async-done(((f32[3,3,256,256]{2,3,1,0:T(8,128)}), f32[3,3,256,256]{2,3,1,0:T(8,128)}) %all-reduce.7.cloned.1.call-update) | async-done | bytes 2359312 | tf_op jit(solution)/shard_map/psum | solution.py:58
  166.7 4.6 broadcast_select_fusion
  173.6 11.7 %cholesky.172 = f32[128,128]{1,0:T(8,128)S(1)} custom-call(f32[128,128]{1,0:T(8,128)S(1)} %cholesky.270), custom_call_target="Cholesky" | custom-call | tf_op jit(solution)/shard_map/jit(cholesky)/cholesky | solution.py:99
  185.4 9.8 %custom-call.15 = f32[1,128,128]{1,2,0:T(8,128)S(1)} custom-call(f32[1,128,128]{2,1,0:T(8,128)S(1)} %get-tuple-element.105), custom_call_target="InvertDiagBlocksLowerTriangular" | custom-call | tf_op jit(solution)/shard_map/jit(cholesky)/cholesky | solution.py:99
  195.7 11.7 %cholesky.189 = f32[128,128]{1,0:T(8,128)S(1)} custom-call(f32[128,128]{1,0:T(8,128)S(1)} %convolution_subtract_fusion.15), custom_call_target="Cholesky" | custom-call | tf_op jit(solution)/shard_map/jit(cholesky)/cholesky | solution.py:99
  210.1 3.8 while.6
  214.0 20.1 %custom-call.16 = f32[2,128,128]{1,2,0:T(8,128)S(1)} custom-call(f32[2,128,128]{2,1,0:T(8,128)S(1)} %get-tuple-element.28), custom_call_target="InvertDiagBlocksLowerTriangular" | custom-call | tf_op jit(solution)/shard_map/jit(_solve_triangular)/triangular_solve | solution.py:101
  235.0 1.6 fusion.20
  238.1 11.7 %cholesky.206 = f32[128,128]{1,0:T(8,128)S(1)} custom-call(f32[128,128]{1,0:T(8,128)S(1)} %cholesky.273), custom_call_target="Cholesky" | custom-call | tf_op jit(solution)/shard_map/jit(cholesky)/cholesky | solution.py:99
  249.9 9.8 %custom-call.17 = f32[1,128,128]{1,2,0:T(8,128)S(1)} custom-call(f32[1,128,128]{2,1,0:T(8,128)S(1)} %get-tuple-element.101), custom_call_target="InvertDiagBlocksLowerTriangular" | custom-call | tf_op jit(solution)/shard_map/jit(cholesky)/cholesky | solution.py:99
  260.2 11.7 %cholesky.223 = f32[128,128]{1,0:T(8,128)S(1)} custom-call(f32[128,128]{1,0:T(8,128)S(1)} %convolution_subtract_fusion.14), custom_call_target="Cholesky" | custom-call | tf_op jit(solution)/shard_map/jit(cholesky)/cholesky | solution.py:99
  275.4 4.2 while.7
  279.6 19.9 %custom-call.18 = f32[2,128,128]{1,2,0:T(8,128)S(1)} custom-call(f32[2,128,128]{2,1,0:T(8,128)S(1)} %get-tuple-element.29), custom_call_target="InvertDiagBlocksLowerTriangular" | custom-call | tf_op jit(solution)/shard_map/jit(_solve_triangular)/triangular_solve | solution.py:101
  302.6 2.2 convolution_subtract_fusion.8
  304.8 20.6 %all-reduce.9.cloned.1.call-done = f32[16,256,256]{1,2,0:T(8,128)} async-done(((f32[16,256,256]{1,2,0:T(8,128)}), f32[16,256,256]{1,2,0:T(8,128)}) %all-reduce.9.cloned.1.call-update) | async-done | bytes 4194320 | tf_op jit(solution)/shard_map/psum | solution.py:69
  326.8 2.5 slice_bitcast_fusion.1
  329.4 3.6 fusion.4
  333.2 2.4 copy-done.12
  336.6 4.7 maximum_bitcast_fusion
  345.1 11.7 %cholesky.240 = f32[128,128]{1,0:T(8,128)S(1)} custom-call(f32[128,128]{1,0:T(8,128)S(1)} %cholesky.276), custom_call_target="Cholesky" | custom-call | tf_op jit(solution)/shard_map/jit(cholesky)/cholesky | solution.py:99
  356.9 10.2 %custom-call.19 = f32[1,128,128]{1,2,0:T(8,128)S(1)} custom-call(f32[1,128,128]{2,1,0:T(8,128)S(1)} %get-tuple-element.97), custom_call_target="InvertDiagBlocksLowerTriangular" | custom-call | tf_op jit(solution)/shard_map/jit(cholesky)/cholesky | solution.py:99
  367.5 11.7 %cholesky.257 = f32[128,128]{1,0:T(8,128)S(1)} custom-call(f32[128,128]{1,0:T(8,128)S(1)} %convolution_subtract_fusion.13), custom_call_target="Cholesky" | custom-call | tf_op jit(solution)/shard_map/jit(cholesky)/cholesky | solution.py:99
  382.7 4.0 while.8
  386.6 20.3 %custom-call.20 = f32[2,128,128]{1,2,0:T(8,128)} custom-call(f32[2,128,128]{2,1,0:T(8,128)S(1)} %get-tuple-element.30), custom_call_target="InvertDiagBlocksLowerTriangular" | custom-call | tf_op jit(solution)/shard_map/jit(_solve_triangular)/triangular_solve | solution.py:101
  408.3 2.3 copy.98
  410.6 1.9 convolution_subtract_fusion.4
  412.6 2.0 bitcast_select_fusion.1
  414.6 2.5 copy.102
  417.0 1.8 copy.92
  424.1 1.7 bitcast_select_fusion
  427.0 51.3 %all-reduce.11.cloned.1.call-done = f32[3,256,12,256]{1,3,2,0:T(8,128)} async-done(((f32[3,256,12,256]{1,3,2,0:T(8,128)}), f32[3,256,12,256]{1,3,2,0:T(8,128)}) %all-reduce.11.cloned.1.call-update) | async-done | bytes 9437200 | tf_op jit(solution)/shard_map/psum | solution.py:88
  478.3 7.5 %fusion.83 = (f32[1,256,12,256]{1,3,2,0:T(8,128)}, f32[1,256,12,256]{1,3,2,0:T(8,128)S(1)}, f32[1,256,12,256]{1,3,2,0:T(8,128)}) fusion(f32[3,256,12,256]{1,3,2,0:T(8,128)} %all-reduce.11.cloned.1.call-done), kind=kLoop, calls=%fused_computation.179 | loop fusion | bytes 18874368 | tf_op jit(solution)/shard_map/slice | solution.py:119
  485.8 2.3 copy.105
  488.1 4.8 fusion.37
  492.9 3.7 copy.104
  496.6 5.2 convolution_subtract_fusion.1
  501.8 3.0 convolution_subtract_fusion.2
  504.9 3.0 fusion.34
  507.9 3.0 convolution_subtract_fusion
  510.9 4.7 fusion.32
  515.6 7.7 %pad_maximum_fusion = f32[768,3072]{1,0:T(8,128)} fusion(f32[256,3072]{1,0:T(8,128)} %fusion.32, f32[256,3072]{1,0:T(8,128)} %copy-done, f32[256,3072]{1,0:T(8,128)S(1)} %fusion.37), kind=kLoop, calls=%fused_computation.7 | loop fusion | flops 4718592 | bytes 18874368 | tf_op jit(solution)/shard_map/concatenate | solution.py:125
  523.3 10.0 %fusion.2 = f32[768,1536]{1,0:T(8,128)} fusion(f32[768,3072]{1,0:T(8,128)} %pad_maximum_fusion, f32[768,256]{1,0:T(8,128)} %get-tuple-element.114, f32[768,256]{1,0:T(8,128)} %get-tuple-element.112, f32[768,256]{1,0:T(8,128)} %bitcast.226), kind=kOutput, calls=%fused_computation.11 | convolution fusion | flops 5436997632 | bytes 11796480 | tf_op jit(solution)/shard_map/dot_general | solution.py:16
  533.3 7.7 %fusion = f32[768,1536]{1,0:T(8,128)} fusion(f32[768,3072]{1,0:T(8,128)S(1)} %copy-done.5, f32[768,256]{1,0:T(8,128)S(1)} %copy-done.39, f32[768,256]{1,0:T(8,128)S(1)} %copy-done.24, f32[768,256]{1,0:T(8,128)S(1)} %bitcast.227), kind=kOutput, calls=%fused_computation.9 | convolution fusion | flops 5436997632 | bytes 11796480 | tf_op jit(solution)/shard_map/dot_general | solution.py:16
  541.0 6.9 %reshape.317 = f32[3,256,6,256]{3,2,1,0:T(8,128)} reshape(f32[768,1536]{1,0:T(8,128)} %fusion.2) | data formatting | bytes 9437184 | tf_op jit(solution)/shard_map/reshape | solution.py:128
  547.9 6.0 %copy.106 = f32[3,256,6,256]{1,3,2,0:T(8,128)} copy(f32[3,256,6,256]{3,2,1,0:T(8,128)} %reshape.317) | data formatting | bytes 9437184 | tf_op jit(solution)/shard_map/reshape | solution.py:128
  553.9 4.4 bitcast_subtract_fusion
  560.6 2.7 fusion.5
  563.3 12.1 %copy.109 = f32[1,3,256,1,6,256]{5,3,4,2,1,0:T(1,128)} copy(f32[1,3,256,1,6,256]{2,5,4,1,3,0:T(8,128)} %fusion.5) | data formatting | bytes 9437184
  575.4 7.1 %reshape.319 = f32[1,3,256,6,256]{4,3,2,1,0:T(8,128)} reshape(f32[768,1536]{1,0:T(8,128)} %fusion) | data formatting | bytes 9437184 | tf_op jit(solution)/shard_map/reshape | solution.py:129
  582.5 7.2 %copy_subtract_fusion = f32[1,3,256,6,256]{4,3,2,1,0:T(8,128)S(1)} fusion(f32[1,3,256,6,256]{4,3,2,1,0:T(8,128)} %reshape.319, f32[1,3,256,6,256]{4,2,3,1,0:T(8,128)} %param.7), kind=kLoop, calls=%fused_computation.8 | loop fusion | flops 1179648 | bytes 14155776 | tf_op jit(solution)/shard_map/sub | solution.py:130
  589.7 3.6 copy.110
  (235 shorter events, 57.1 us)
Async XLA Ops:
  7.2 80.9 %all-gather.3.cloned.1.call-start = ((), (), s32[]{:S(2)}) async-start(), calls=%async_computation.3 | async-start | bytes 3932160 | tf_op jit(solution)/shard_map/all_gather | solution.py:35
  19.3 3.1 copy-start.54
  21.7 145.0 %all-reduce.7.cloned.1.call-start = ((), (), s32[]{:S(2)}) async-start(), calls=%async_computation | async-start | bytes 4718592 | tf_op jit(solution)/shard_map/psum | solution.py:58
  42.7 0.6 copy-start.40
  42.7 1.7 copy-start.42
  43.4 0.9 copy-start.44
  43.4 0.9 copy-start.46
  88.0 5.6 copy-start.3
  96.2 4.2 copy-start.21
  98.5 3.0 copy-start.49
  104.9 220.5 %all-reduce.9.cloned.1.call-start = ((), (), s32[]{:S(2)}) async-start(), calls=%async_computation.1 | async-start | bytes 8388608 | tf_op jit(solution)/shard_map/psum | solution.py:69
  105.0 194.8 %copy-start.13 = (f32[256,256]{1,0:T(8,128)}, f32[256,256]{1,0:T(8,128)S(1)}, u32[]{:S(2)}) copy-start(f32[256,256]{1,0:T(8,128)S(1)} %fusion.31) | copy-start | bytes 786436
  171.3 307.1 %all-reduce.11.cloned.1.call-start = ((), (), s32[]{:S(2)}) async-start(), calls=%async_computation.2 | async-start | bytes 18874368 | tf_op jit(solution)/shard_map/psum | solution.py:88
  235.0 172.1 %copy-start.18 = (f32[128,256]{1,0:T(8,128)}, f32[128,256]{1,0:T(8,128)S(1)}, u32[]{:S(2)}) copy-start(f32[128,256]{1,0:T(8,128)S(1)} %fusion.53) | copy-start | bytes 393220
  279.6 45.7 %copy-start.52 = (s32[2,2]{1,0:T(2,128)}, s32[2,2]{1,0:T(2,128)S(1)}, u32[]{:S(2)}) copy-start(s32[2,2]{1,0:T(2,128)S(1)} %get-tuple-element.277) | copy-start | bytes 52
  299.8 41.5 %copy-start.15 = (f32[128,256]{1,0:T(8,128)}, f32[128,256]{1,0:T(8,128)S(1)}, u32[]{:S(2)}) copy-start(f32[128,256]{1,0:T(8,128)S(1)} %fusion.40) | copy-start | bytes 393220
  302.6 119.8 %copy-start.4 = (f32[256,256]{1,0:T(8,128)}, f32[256,256]{1,0:T(8,128)S(1)}, u32[]{:S(2)}) copy-start(f32[256,256]{1,0:T(8,128)S(1)} %fusion.22) | copy-start | bytes 786436
  325.4 4.0 slice-start
  326.8 2.5 slice-start.1
  333.0 3.7 copy-start.1
  333.0 2.6 copy-start.12
  341.3 0.9 copy-start.29
  341.3 1.0 copy-start.37
  342.4 40.3 %copy-start.53 = (s32[2,2]{1,0:T(2,128)S(1)}, s32[2,2]{1,0:T(2,128)}, u32[]{:S(2)}) copy-start(s32[2,2]{1,0:T(2,128)} %copy-done.52) | copy-start | bytes 52
  343.0 80.3 %copy-start.10 = (f32[256,256]{1,0:T(8,128)}, f32[256,256]{1,0:T(8,128)S(1)}, u32[]{:S(2)}) copy-start(f32[256,256]{1,0:T(8,128)S(1)} %fusion.36) | copy-start | bytes 786436
  343.0 64.0 %copy-start.38 = (f32[256,256]{1,0:T(8,128)S(1)}, f32[256,256]{1,0:T(8,128)}, u32[]{:S(2)}) copy-start(f32[256,256]{1,0:T(8,128)} %get-tuple-element.68) | copy-start | bytes 786436
  344.5 62.6 %copy-start.50 = (pred[3]{0:T(512)(128)(4,1)S(1)}, pred[3]{0:T(512)(128)(4,1)}, u32[]{:S(2)}) copy-start(pred[3]{0:T(512)(128)(4,1)} %get-tuple-element.116) | copy-start | bytes 13
  344.5 62.6 %copy-start.51 = (pred[3]{0:T(512)(128)(4,1)S(1)}, pred[3]{0:T(512)(128)(4,1)}, u32[]{:S(2)}) copy-start(pred[3]{0:T(512)(128)(4,1)} %get-tuple-element.117) | copy-start | bytes 13
  386.6 20.4 %copy-start.32 = (f32[256,256]{1,0:T(8,128)}, f32[256,256]{1,0:T(8,128)S(1)}, u32[]{:S(2)}) copy-start(f32[256,256]{1,0:T(8,128)S(1)} %get-tuple-element.272) | copy-start | bytes 786436
  408.0 6.6 %copy-start.6 = (f32[3,256,256]{1,2,0:T(8,128)}, f32[3,256,256]{1,2,0:T(8,128)S(1)}, u32[]{:S(2)}) copy-start(f32[3,256,256]{1,2,0:T(8,128)S(1)} %fusion.9) | copy-start | bytes 2359300
  408.0 4.6 copy-start.16
  408.0 4.6 copy-start.25
  408.0 4.6 copy-start.30
  408.3 14.1 %copy-start.8 = (f32[3,256,256]{2,1,0:T(8,128)}, f32[3,256,256]{2,1,0:T(8,128)S(1)}, u32[]{:S(2)}) copy-start(f32[3,256,256]{2,1,0:T(8,128)S(1)} %copy.97) | copy-start | bytes 2359300
  412.6 6.3 %copy-start.14 = (f32[256,256]{1,0:T(8,128)S(1)}, f32[256,256]{1,0:T(8,128)}, u32[]{:S(2)}) copy-start(f32[256,256]{1,0:T(8,128)} %copy-done.13) | copy-start | bytes 786436
  414.6 7.8 %copy-start.22 = (f32[3,1,256,256]{3,2,0,1:T(8,128)S(1)}, f32[3,1,256,256]{3,2,0,1:T(8,128)}, u32[]{:S(2)}) copy-start(f32[3,1,256,256]{3,2,0,1:T(8,128)} %copy.93) | copy-start | bytes 2359300
  414.6 8.7 %copy-start.23 = (f32[768,256]{1,0:T(8,128)S(1)}, f32[768,256]{1,0:T(8,128)}, u32[]{:S(2)}) copy-start(f32[768,256]{1,0:T(8,128)} %get-tuple-element.112) | copy-start | bytes 2359300
  418.9 5.2 copy-start.26
  420.1 5.7 copy-start.27
  422.4 3.4 copy-start.33
  496.6 5.2 copy-start.2
  501.8 3.0 copy-start.17
  501.8 3.0 copy-start.31
  504.8 3.0 copy-start.11
  507.8 3.1 copy-start
  507.8 3.1 copy-start.28
  507.8 3.1 copy-start.34
  523.3 10.0 %copy-start.5 = (f32[768,3072]{1,0:T(8,128)S(1)}, f32[768,3072]{1,0:T(8,128)}, u32[]{:S(2)}) copy-start(f32[768,3072]{1,0:T(8,128)} %pad_maximum_fusion) | copy-start | bytes 28311556
  523.3 10.0 %copy-start.9 = (f32[3,256,256]{2,1,0:T(8,128)S(1)}, f32[3,256,256]{2,1,0:T(8,128)}, u32[]{:S(2)}) copy-start(f32[3,256,256]{2,1,0:T(8,128)} %copy-done.8) | copy-start | bytes 2359300
  523.3 10.0 %copy-start.24 = (f32[768,256]{1,0:T(8,128)S(1)}, f32[768,256]{1,0:T(8,128)}, u32[]{:S(2)}) copy-start(f32[768,256]{1,0:T(8,128)} %get-tuple-element.112) | copy-start | bytes 2359300
  523.3 10.0 %copy-start.39 = (f32[768,256]{1,0:T(8,128)S(1)}, f32[768,256]{1,0:T(8,128)}, u32[]{:S(2)}) copy-start(f32[768,256]{1,0:T(8,128)} %get-tuple-element.114) | copy-start | bytes 2359300
  558.3 1.1 copy-start.7
  558.3 1.4 copy-start.19
  558.3 1.6 copy-start.20
  558.3 1.6 copy-start.35
  558.3 1.7 copy-start.36
  558.3 1.7 copy-start.41
  558.3 1.7 copy-start.43
  558.4 1.7 copy-start.45
  558.4 1.7 copy-start.47
  560.0 0.6 copy-start.48
Sparse Core Ops, SparseCore 0:
  21.8 66.1 all-gather.2
  105.0 61.5 all-reduce.6
  171.4 153.9 all-reduce.8
  341.5 136.7 all-reduce.10

commit v2 on v1

--- a/solution.py
+++ b/solution.py
@@ -16,6 +16,24 @@
     return lax.dot_general(a, b, (((1,), (0,)), ((), ())), precision=precision)
 
 
+def factor_tile(tile):
+    half = tile.shape[0] // 2
+    identity = jnp.eye(half, dtype=jnp.float32)
+
+    def base(block):
+        lower = jnp.linalg.cholesky(block)
+        return lower, jax.scipy.linalg.solve_triangular(lower, identity, lower=True)
+
+    first, first_inv = base(tile[:half, :half])
+    below = dot_t(tile[half:, :half], first_inv)
+    second, second_inv = base(tile[half:, half:] - dot_t(below, below))
+    below_inv = -dot(second_inv, dot(below, first_inv))
+    zero = jnp.zeros((half, half), jnp.float32)
+    return jnp.block([[first, zero], [below, second]]), jnp.block(
+        [[first_inv, zero], [below_inv, second_inv]]
+    )
+
+
 def shards(matrix, checksum, failed):
     rows_count = lax.axis_size("row")
     cols_count = lax.axis_size("col")
@@ -32,7 +50,31 @@
     lost_column = lax.all_gather(failed, "col", axis=0, tiled=True)[0]
     lost = column_position == lost_column
 
-    gathered = lax.all_gather(own[:, :slots], "col", axis=0)
+    pieces = []
+    pairs = [(i, k) for i in range(PANELS) for k in range(i + 1)]
+    for i, k in pairs:
+        a, b, root = i // rows_count, k // cols_count, k % cols_count
+        rebuilt = jnp.where(lost, totals[a, b], -own[a, b])
+        plain = jnp.where(column_position == root, own[a, b], 0.0)
+        piece = jnp.where(lost_column == root, rebuilt, plain)
+        pieces.append(jnp.where(row_index == i % rows_count, piece, 0.0))
+    lead = lax.psum(jnp.stack(pieces), ("row", "col"))
+
+    need = [
+        min(tile_cols, (rows_count * (a + 1) - 1) // cols_count + 1) for a in range(tile_rows)
+    ]
+    healthy = jnp.where(lost, 0.0, own)
+    top_part = healthy[:top_slots, slots:]
+    rest_part = jnp.concatenate(
+        [healthy[a, slots : need[a]] for a in range(top_slots, tile_rows)], axis=0
+    )
+    front_part = own[:, :slots]
+    lead, top_part, rest_part, front_part = lax.optimization_barrier(
+        (lead, top_part, rest_part, front_part)
+    )
+    lead = dict(zip(pairs, [lead[n] for n in range(len(pairs))]))
+
+    gathered = lax.all_gather(front_part, "col", axis=0)
     ids = jnp.arange(cols_count, dtype=jnp.int32).reshape(-1, 1, 1, 1, 1)
     others = jnp.sum(jnp.where(ids != lost_column, gathered, 0.0), axis=0)
     patch = totals[:, :slots] - others
@@ -42,52 +84,26 @@
         panels.append(
             jnp.where(lost_column == k % cols_count, patch[:, slot], gathered[k % cols_count, :, slot])
         )
+    front_work = jnp.where(lost, patch, own[:, :slots])
 
-    lead = jnp.stack(
-        [
-            jnp.where(
-                row_index == i % rows_count,
-                jnp.stack([panels[k][i // rows_count] for k in range(i + 1)] + [
-                    jnp.zeros((width, width), jnp.float32) for _ in range(i + 1, PANELS)
-                ]),
-                0.0,
-            )
-            for i in range(PANELS)
-        ]
-    )
-    lead = lax.psum(lead, "row")
-
-    need = [
-        tile_cols
-        if a < top_slots
-        else min(tile_cols, (rows_count * (a + 1) - 1) // cols_count + 1)
-        for a in range(tile_rows)
-    ]
-    packed = jnp.concatenate([own[a, : need[a]] for a in range(tile_rows)], axis=0)
-    lead_done, packed = lax.optimization_barrier((lead, packed))
-    lead = lead_done
-    summed = lax.psum(jnp.where(lost, 0.0, packed), "col")
-    filled = []
-    start = 0
-    for a in range(tile_rows):
-        pad = jnp.zeros((tile_cols - need[a], width, width), jnp.float32)
-        filled.append(jnp.concatenate([summed[start : start + need[a]], pad], axis=0))
-        start += need[a]
-    work = jnp.where(lost, totals - jnp.stack(filled), own)
+    top_sum = lax.psum(top_part, "col")
+    top_back = jnp.where(lost, totals[:top_slots, slots:] - top_sum, own[:top_slots, slots:])
+    top_work = jnp.concatenate([front_work[:top_slots], top_back], axis=1)
 
     tops = jnp.stack(
         [
             jnp.where(
                 row_index == i % rows_count,
-                jnp.concatenate([work[i // rows_count], totals[i // rows_count]], axis=0),
+                jnp.concatenate([top_work[i // rows_count], totals[i // rows_count]], axis=0),
                 0.0,
             )
             for i in range(PANELS)
         ]
     )
     tops = lax.psum(tops, "row")
+    tops, rest_part = lax.optimization_barrier((tops, rest_part))
+    rest_sum = lax.psum(rest_part, "col")
 
-    identity = jnp.eye(width, dtype=jnp.float32)
     factor = {}
     inverse = []
     for k in range(PANELS):
@@ -96,10 +112,8 @@
             for m in range(k):
                 tile = tile - dot_t(factor[i, m], factor[k, m])
             if i == k:
-                factor[k, k] = jnp.linalg.cholesky(tile)
-                inverse.append(
-                    jax.scipy.linalg.solve_triangular(factor[k, k], identity, lower=True)
-                )
+                factor[k, k], made = factor_tile(tile)
+                inverse.append(made)
             else:
                 factor[i, k] = dot_t(tile, inverse[k])
 
@@ -129,7 +143,18 @@
     drop = dot(rows_factor, cols_factor[:, split:], FAST).reshape(shape).transpose(0, 2, 1, 3)
     new_totals = (totals - drop).transpose(0, 2, 1, 3)
 
-    work = work - update
+    filled = []
+    start = 0
+    for a in range(top_slots, tile_rows):
+        count = need[a] - slots
+        pad = jnp.zeros((tile_cols - need[a], width, width), jnp.float32)
+        filled.append(jnp.concatenate([rest_sum[start : start + count], pad], axis=0))
+        start += count
+    rest_back = jnp.where(
+        lost, totals[top_slots:, slots:] - jnp.stack(filled), own[top_slots:, slots:]
+    )
+    rest_work = jnp.concatenate([front_work[top_slots:], rest_back], axis=1)
+    work = jnp.concatenate([top_work, rest_work], axis=0) - update
     front = []
     for b in range(slots):
         tiles = work[:, b]

time: 607 us -> 593 us (0.977)
  other arithmetic: 213 us -> 203 us
  local copies, waits for them, and re-layouts: 122 us -> 112 us
  waiting for transfers between devices: 168 us -> 177 us
    psum x2 -> x3, waiting for transfers between devices: 73.2 us -> 117 us  [the longest x1 117 us: shards(): lead = lax.psum(jnp.stack(pieces), ('row', 'col'))]
    all_gather x1, waiting for transfers between devices: 43.6 us -> 17 us  [shards(): gathered = lax.all_gather(front_part, 'col', axis=0)]
    another operation x30 -> x3, local copies, waits for them, and re-layouts: 14.6 us -> 1.52 us  [base(): jax.scipy.linalg.solve_triangular(lower, identity, lower=True)]
    another operation x28 -> x33, other arithmetic: 168 us -> 156 us  [the longest x18 77.7 us: base(): lower = jnp.linalg.cholesky(block)]
    psum x1, waiting for transfers between devices: 51.3 us -> 42.7 us  [shards(): tops = lax.psum(tops, 'row')]
    dot_general x8 -> x14, matrix products: 41.3 us -> 47.2 us  [dot(): return lax.dot_general(a, b, (((1,), (0,)), ((), ())), precision=precision)]
    unnamed x124 -> x136, local copies, waits for them, and re-layouts: 46.6 us -> 45.5 us
    dot_general x13 -> x19, matrix products: 17.3 us -> 18.1 us  [dot_t(): return lax.dot_general(a, b, (((1,), (1,)), ((), ())), precision=precision)]
  transfers between devices with their start and end apart: 4 -> 5, of which waited for: 4 -> 3; matrix products, arithmetic and copies ran while one was open for 39% -> 53% of each run, Pallas kernels for 0% -> 0%
where the time goes in v2:
time: 593 us; the launch traced here: 588 us
  other arithmetic  203 us (34%)
  waiting for transfers between devices  177 us (30%)
  local copies, waits for them, and re-layouts  112 us (19%)
  matrix products  68.7 us (12%)
  between operations  16 us (3%)
  blocking collectives  9.92 us (2%)
    psum x1, waiting for transfers between devices, shards(): lead = lax.psum(jnp.stack(pieces), ('row', 'col'))  117 us
    another operation x18, other arithmetic, base(): lower = jnp.linalg.cholesky(block)  77.7 us
    another operation x12, other arithmetic, base(): jax.scipy.linalg.solve_triangular(lower, identity, lower=True)  70.2 us
    dot_general x14, matrix products, dot(): return lax.dot_general(a, b, (((1,), (0,)), ((), ())), precision=precision)  47.2 us
    unnamed x136, local copies, waits for them, and re-layouts  45.5 us
    psum x1, waiting for transfers between devices, shards(): tops = lax.psum(tops, 'row')  42.7 us
    dot_general x19, matrix products, dot_t(): return lax.dot_general(a, b, (((1,), (1,)), ((), ())), precision=precision)  18.1 us
    all_gather x1, waiting for transfers between devices, shards(): gathered = lax.all_gather(front_part, 'col', axis=0)  17 us
  transfers between devices with their start and end apart: 5, of which 3 were waited for; matrix products, arithmetic and copies ran while one was open for 53% of the time, Pallas kernels for 0%

profile of v2, /device:TPU:0, one launch (start us, length us, event | category | flops | bytes accessed | tf_op | source)
XLA Modules:
  0.0 587.9 jit_solution(15508481146544612879)
XLA Ops:
  9.9 9.9 %all-reduce.6 = s32[4]{0:T(128)S(1)} all-reduce(s32[4]{0:T(128)S(1)} %dynamic-update-slice.2), channel_id=1, replica_groups=mesh['row'=8,'col'=4] {'col'}, use_global_device_ids=true, to_apply=%add.6 | all-reduce | flops 4 | bytes 32
  20.0 12.1 %copy.124 = f32[1,3,256,1,6,256]{2,5,4,1,3,0:T(8,128)} copy(f32[1,3,256,1,6,256]{5,3,4,2,1,0:T(1,128)} %param.6) | data formatting | bytes 9437184 | tf_op args[0]
  32.0 6.1 %copy.123 = f32[1,3,256,6,256]{2,4,3,1,0:T(8,128)} copy(f32[1,3,256,6,256]{4,2,3,1,0:T(8,128)} %param.7) | data formatting | bytes 9437184 | tf_op args[1]
  43.7 2.8 slice.226
  46.5 2.9 broadcast_select_fusion
  49.5 1.8 slice.207
  53.0 3.1 slice_bitcast_fusion.1
  56.1 1.6 pad_maximum_fusion.4
  58.3 117.3 %all-reduce.12.cloned.1.call-done = f32[6,256,256]{1,2,0:T(8,128)} async-done(((f32[6,256,256]{1,2,0:T(8,128)}), f32[6,256,256]{1,2,0:T(8,128)}) %all-reduce.12.cloned.1.call-update) | async-done | bytes 1572880 | tf_op jit(solution)/shard_map/psum | solution.py:61
  178.1 11.7 %cholesky.104 = f32[128,128]{1,0:T(8,128)S(1)} custom-call(f32[128,128]{1,0:T(8,128)S(1)} %fusion.59), custom_call_target="Cholesky" | custom-call | tf_op jit(solution)/shard_map/jit(cholesky)/cholesky | solution.py:24
  191.8 9.8 %custom-call.10 = f32[1,128,128]{1,2,0:T(8,128)S(1)} custom-call(f32[1,128,128]{2,1,0:T(8,128)S(1)} %get-tuple-element.36), custom_call_target="InvertDiagBlocksLowerTriangular" | custom-call | tf_op jit(solution)/shard_map/jit(_solve_triangular)/triangular_solve | solution.py:25
  203.2 11.7 %cholesky.115 = f32[128,128]{1,0:T(8,128)S(1)} custom-call(f32[128,128]{1,0:T(8,128)S(1)} %fusion.57), custom_call_target="Cholesky" | custom-call | tf_op jit(solution)/shard_map/jit(cholesky)/cholesky | solution.py:24
  215.7 1.3 fusion.77
  217.0 10.0 %custom-call.11 = f32[1,128,128]{1,2,0:T(8,128)S(1)} custom-call(f32[1,128,128]{2,1,0:T(8,128)S(1)} %get-tuple-element.34), custom_call_target="InvertDiagBlocksLowerTriangular" | custom-call | tf_op jit(solution)/shard_map/jit(_solve_triangular)/triangular_solve | solution.py:25
  229.2 11.7 %cholesky.126 = f32[128,128]{1,0:T(8,128)S(1)} custom-call(f32[128,128]{1,0:T(8,128)S(1)} %fusion.55), custom_call_target="Cholesky" | custom-call | tf_op jit(solution)/shard_map/jit(cholesky)/cholesky | solution.py:24
  242.8 9.8 %custom-call.12 = f32[1,128,128]{1,2,0:T(8,128)S(1)} custom-call(f32[1,128,128]{2,1,0:T(8,128)S(1)} %get-tuple-element.32), custom_call_target="InvertDiagBlocksLowerTriangular" | custom-call | tf_op jit(solution)/shard_map/jit(_solve_triangular)/triangular_solve | solution.py:25
  254.3 11.7 %cholesky.137 = f32[128,128]{1,0:T(8,128)S(1)} custom-call(f32[128,128]{1,0:T(8,128)S(1)} %fusion.53), custom_call_target="Cholesky" | custom-call | tf_op jit(solution)/shard_map/jit(cholesky)/cholesky | solution.py:24
  267.8 10.1 %custom-call.13 = f32[1,128,128]{1,2,0:T(8,128)S(1)} custom-call(f32[1,128,128]{2,1,0:T(8,128)S(1)} %get-tuple-element.30), custom_call_target="InvertDiagBlocksLowerTriangular" | custom-call | tf_op jit(solution)/shard_map/jit(_solve_triangular)/triangular_solve | solution.py:25
  283.0 2.4 slice_select_fusion.2
  285.4 17.0 %all-gather.3.cloned.1.call-done = f32[12,1,256,256]{3,2,1,0:T(8,128)} async-done(((f32[3,1,256,256]{3,2,1,0:T(8,128)}), f32[12,1,256,256]{3,2,1,0:T(8,128)}) %all-gather.3.cloned.1.call-update) | async-done | bytes 3145744 | tf_op jit(solution)/shard_map/all_gather | solution.py:77
  302.4 2.7 fusion.115
  305.1 2.3 copy.185
  307.4 3.2 select_reduce_fusion
  310.6 2.3 copy.145
  314.0 2.7 broadcast_select_fusion.4
  316.8 2.3 broadcast_select_fusion.5
  320.2 4.7 pad_maximum_fusion
  327.8 13.2 %cholesky.148 = f32[128,128]{1,0:T(8,128)} custom-call(f32[128,128]{1,0:T(8,128)} %fusion.51), custom_call_target="Cholesky" | custom-call | tf_op jit(solution)/shard_map/jit(cholesky)/cholesky | solution.py:24
  342.6 2.2 select_bitcast_fusion.1
  344.7 11.3 %custom-call.14 = f32[1,128,128]{1,2,0:T(8,128)} custom-call(f32[1,128,128]{2,1,0:T(8,128)} %get-tuple-element.28), custom_call_target="InvertDiagBlocksLowerTriangular" | custom-call | tf_op jit(solution)/shard_map/jit(_solve_triangular)/triangular_solve | solution.py:25
  360.8 12.6 %cholesky.159 = f32[128,128]{1,0:T(8,128)S(1)} custom-call(f32[128,128]{1,0:T(8,128)} %fusion.49), custom_call_target="Cholesky" | custom-call | tf_op jit(solution)/shard_map/jit(cholesky)/cholesky | solution.py:24
  375.3 10.8 %custom-call.15 = f32[1,128,128]{1,2,0:T(8,128)} custom-call(f32[1,128,128]{2,1,0:T(8,128)S(1)} %get-tuple-element.26), custom_call_target="InvertDiagBlocksLowerTriangular" | custom-call | tf_op jit(solution)/shard_map/jit(_solve_triangular)/triangular_solve | solution.py:25
  387.9 1.6 select_maximum_fusion.2
  389.5 1.8 copy.149
  396.0 1.7 convolution_negate_fusion
  397.8 1.9 slice.224
  402.1 1.9 fusion.6
  404.3 2.6 copy.158
  406.9 2.0 convolution_subtract_fusion.4
  408.9 2.9 bitcast_select_fusion.1
  411.8 2.4 copy.162
  415.9 1.7 bitcast_select_fusion
  418.9 42.7 %all-reduce.16.cloned.1.call-done = f32[3,12,256,256]{2,3,1,0:T(8,128)} async-done(((f32[3,12,256,256]{2,3,1,0:T(8,128)}), f32[3,12,256,256]{2,3,1,0:T(8,128)}) %all-reduce.16.cloned.1.call-update) | async-done | bytes 9437200 | tf_op jit(solution)/shard_map/psum | solution.py:103
  461.6 7.4 %fusion.114 = (f32[1,256,12,256]{1,3,2,0:T(8,128)}, f32[1,256,12,256]{1,3,2,0:T(8,128)S(1)}, f32[1,256,12,256]{1,3,2,0:T(8,128)}) fusion(f32[3,256,12,256]{1,3,2,0:T(8,128)} %bitcast.210), kind=kLoop, calls=%fused_computation.202 | loop fusion | bytes 18874368 | tf_op jit(solution)/shard_map/slice | solution.py:133
  469.0 2.3 copy.165
  471.4 4.8 fusion.80
  476.1 3.8 copy.164
  479.9 5.2 convolution_subtract_fusion.1
  485.1 3.0 convolution_subtract_fusion.2
  488.2 2.9 fusion.39
  491.1 3.0 convolution_subtract_fusion
  494.2 4.7 fusion.33
  498.9 7.6 %pad_maximum_fusion.1 = f32[768,3072]{1,0:T(8,128)} fusion(f32[256,3072]{1,0:T(8,128)} %fusion.33, f32[256,3072]{1,0:T(8,128)} %copy-done, f32[256,3072]{1,0:T(8,128)S(1)} %fusion.80), kind=kLoop, calls=%fused_computation.1 | loop fusion | flops 4718592 | bytes 18874368 | tf_op jit(solution)/shard_map/concatenate | solution.py:139
  506.6 9.8 %fusion.2 = f32[768,1536]{1,0:T(8,128)} fusion(f32[768,3072]{1,0:T(8,128)} %pad_maximum_fusion.1, f32[768,256]{1,0:T(8,128)} %get-tuple-element.57, f32[768,256]{1,0:T(8,128)} %get-tuple-element.55, f32[768,256]{1,0:T(8,128)} %bitcast.213), kind=kOutput, calls=%fused_computation.5 | convolution fusion | flops 5436997632 | bytes 11796480 | tf_op jit(solution)/shard_map/dot_general | solution.py:16
  516.4 7.0 %reshape.402 = f32[3,256,6,256]{3,2,1,0:T(8,128)} reshape(f32[768,1536]{1,0:T(8,128)} %fusion.2) | data formatting | bytes 9437184 | tf_op jit(solution)/shard_map/reshape | solution.py:142
  523.4 6.3 %copy.166 = f32[3,256,6,256]{1,3,2,0:T(8,128)} copy(f32[3,256,6,256]{3,2,1,0:T(8,128)} %reshape.402) | data formatting | bytes 9437184 | tf_op jit(solution)/shard_map/reshape | solution.py:142
  529.7 9.2 %fusion = f32[768,1536]{1,0:T(8,128)} fusion(f32[768,3072]{1,0:T(8,128)} %pad_maximum_fusion.1, f32[768,256]{1,0:T(8,128)S(1)} %copy-done.45, f32[768,256]{1,0:T(8,128)S(1)} %copy-done.20, f32[768,256]{1,0:T(8,128)S(1)} %bitcast.214), kind=kOutput, calls=%fused_computation.3 | convolution fusion | flops 5436997632 | bytes 11796480 | tf_op jit(solution)/shard_map/dot_general | solution.py:16
  538.8 7.1 %reshape.404 = f32[1,3,256,6,256]{4,3,2,1,0:T(8,128)} reshape(f32[768,1536]{1,0:T(8,128)} %fusion) | data formatting | bytes 9437184 | tf_op jit(solution)/shard_map/reshape | solution.py:143
  546.0 7.2 %copy_subtract_fusion = f32[1,3,256,6,256]{4,3,2,1,0:T(8,128)S(1)} fusion(f32[1,3,256,6,256]{4,3,2,1,0:T(8,128)} %reshape.404, f32[1,3,256,6,256]{4,2,3,1,0:T(8,128)} %param.7), kind=kLoop, calls=%fused_computation.2 | loop fusion | flops 1179648 | bytes 14155776 | tf_op jit(solution)/shard_map/sub | solution.py:144
  553.2 3.6 copy.170
  556.8 1.9 fusion.5
  558.8 3.2 slice_select_fusion
  566.3 2.7 fusion.4
  569.0 12.1 %copy.169 = f32[1,3,256,1,6,256]{5,3,4,2,1,0:T(1,128)} copy(f32[1,3,256,1,6,256]{2,5,4,1,3,0:T(8,128)} %fusion.4) | data formatting | bytes 9437184
  (243 shorter events, 58.8 us)
Async XLA Ops:
  7.2 168.4 %all-reduce.12.cloned.1.call-start = ((), (), s32[]{:S(2)}) async-start(), calls=%async_computation | async-start | bytes 3145728 | tf_op jit(solution)/shard_map/psum | solution.py:61
  42.5 1.2 copy-start.27
  43.7 239.3 %all-reduce.14.cloned.1.call-start = ((), (), s32[]{:S(2)}) async-start(), calls=%async_computation.1 | async-start | bytes 2621440 | tf_op jit(solution)/shard_map/psum | solution.py:89
  49.5 3.0 copy-start.1
  51.9 4.2 copy-start.53
  52.5 3.6 copy-start.55
  52.5 3.6 copy-start.57
  175.6 52.5 %copy-start.35 = (f32[6,256,256]{1,2,0:T(8,128)S(1)}, f32[6,256,256]{1,2,0:T(8,128)}, u32[]{:S(2)}) copy-start(f32[6,256,256]{1,2,0:T(8,128)} %all-reduce.12.cloned.1.call-done) | copy-start | bytes 4718596
  175.6 126.8 %all-gather.3.cloned.1.call-start = ((), (), s32[]{:S(2)}) async-start(), calls=%async_computation.4 | async-start | bytes 3932160 | tf_op jit(solution)/shard_map/all_gather | solution.py:77
  227.4 53.4 %copy-start.32 = (f32[128,128]{1,0:T(8,128)}, f32[128,128]{1,0:T(8,128)S(1)}, u32[]{:S(2)}) copy-start(f32[128,128]{1,0:T(8,128)S(1)} %copy.129) | copy-start | bytes 196612
  227.4 234.1 %all-reduce.16.cloned.1.call-start = ((), (), s32[]{:S(2)}) async-start(), calls=%async_computation.2 | async-start | bytes 18874368 | tf_op jit(solution)/shard_map/psum | solution.py:103
  228.1 54.9 %copy-start.33 = (f32[128,128]{1,0:T(8,128)}, f32[128,128]{1,0:T(8,128)S(1)}, u32[]{:S(2)}) copy-start(f32[128,128]{1,0:T(8,128)S(1)} %convolution_negate_fusion.2) | copy-start | bytes 196612
  280.8 133.4 %copy-start.5 = (f32[256,256]{1,0:T(8,128)}, f32[256,256]{1,0:T(8,128)S(1)}, u32[]{:S(2)}) copy-start(f32[256,256]{1,0:T(8,128)S(1)} %fusion.17) | copy-start | bytes 786436
  285.4 33.7 %copy-start.3 = (f32[1,5,256,256]{2,3,1,0:T(8,128)}, f32[1,5,256,256]{2,3,1,0:T(8,128)S(1)}, u32[]{:S(2)}) copy-start(f32[1,5,256,256]{2,3,1,0:T(8,128)S(1)} %slice_select_fusion.2) | copy-start | bytes 3932164
  314.0 2.7 copy-start.17
  316.8 2.4 copy-start.12
  319.1 1.1 copy-start.18
  319.1 1.1 copy-start.21
  324.9 0.9 copy-start.38
  324.9 1.0 copy-start.44
  324.9 1.6 copy-start.43
  325.0 231.8 %all-reduce.18.cloned.1.call-start = ((), (), s32[]{:S(2)}) async-start(), calls=%async_computation.3 | async-start | bytes 4194304 | tf_op jit(solution)/shard_map/psum | solution.py:105
  326.6 88.5 %copy-start.10 = (f32[256,256]{1,0:T(8,128)}, f32[256,256]{1,0:T(8,128)S(1)}, u32[]{:S(2)}) copy-start(f32[256,256]{1,0:T(8,128)S(1)} %fusion.41) | copy-start | bytes 786436
  327.0 17.7 %copy-start.42 = (f32[256,256]{0,1:T(8,128)}, f32[256,256]{0,1:T(8,128)S(1)}, u32[]{:S(2)}) copy-start(f32[256,256]{0,1:T(8,128)S(1)} %convolution_subtract_fusion.6) | copy-start | bytes 786436
  327.8 72.0 %copy-start.15 = (f32[3,1,256,256]{2,3,1,0:T(8,128)S(1)}, f32[3,1,256,256]{2,3,1,0:T(8,128)}, u32[]{:S(2)}) copy-start(f32[3,1,256,256]{2,3,1,0:T(8,128)} %get-tuple-element.53) | copy-start | bytes 2359300
  357.1 34.2 %copy-start.29 = (f32[128,128]{1,0:T(8,128)}, f32[128,128]{1,0:T(8,128)S(1)}, u32[]{:S(2)}) copy-start(f32[128,128]{1,0:T(8,128)S(1)} %fusion.23) | copy-start | bytes 196612
  358.2 33.1 %copy-start.34 = (f32[128,128]{0,1:T(8,128)}, f32[128,128]{0,1:T(8,128)S(1)}, u32[]{:S(2)}) copy-start(f32[128,128]{0,1:T(8,128)S(1)} %fusion.42) | copy-start | bytes 196612
  387.2 4.1 copy-start.50
  394.0 9.9 %copy-start.23 = (f32[256,256]{1,0:T(8,128)}, f32[256,256]{1,0:T(8,128)S(1)}, u32[]{:S(2)}) copy-start(f32[256,256]{1,0:T(8,128)S(1)} %select_maximum_fusion.3) | copy-start | bytes 786436
  404.0 7.8 %copy-start.6 = (f32[3,256,256]{1,2,0:T(8,128)}, f32[3,256,256]{1,2,0:T(8,128)S(1)}, u32[]{:S(2)}) copy-start(f32[3,256,256]{1,2,0:T(8,128)S(1)} %fusion.6) | copy-start | bytes 2359300
  404.3 10.0 %copy-start.8 = (f32[3,256,256]{2,1,0:T(8,128)}, f32[3,256,256]{2,1,0:T(8,128)S(1)}, u32[]{:S(2)}) copy-start(f32[3,256,256]{2,1,0:T(8,128)S(1)} %copy.153) | copy-start | bytes 2359300
  404.3 4.7 copy-start.26
  406.9 7.3 %copy-start.16 = (f32[3,1,256,256]{3,2,0,1:T(8,128)S(1)}, f32[3,1,256,256]{3,2,0,1:T(8,128)}, u32[]{:S(2)}) copy-start(f32[3,1,256,256]{3,2,0,1:T(8,128)} %copy.147) | copy-start | bytes 2359300
  411.8 3.3 copy-start.19
  414.2 1.7 copy-start.24
  414.2 1.7 copy-start.30
  414.2 1.7 copy-start.46
  414.2 1.7 copy-start.48
  479.9 5.2 copy-start.2
  485.1 3.0 copy-start.37
  485.1 3.0 copy-start.39
  488.2 2.9 copy-start.11
  491.1 3.1 copy-start
  491.1 3.1 copy-start.31
  491.1 3.1 copy-start.47
  491.1 3.1 copy-start.49
  523.4 6.3 %copy-start.9 = (f32[3,256,256]{2,1,0:T(8,128)S(1)}, f32[3,256,256]{2,1,0:T(8,128)}, u32[]{:S(2)}) copy-start(f32[3,256,256]{2,1,0:T(8,128)} %copy-done.8) | copy-start | bytes 2359300
  523.4 6.3 %copy-start.20 = (f32[768,256]{1,0:T(8,128)S(1)}, f32[768,256]{1,0:T(8,128)}, u32[]{:S(2)}) copy-start(f32[768,256]{1,0:T(8,128)} %get-tuple-element.55) | copy-start | bytes 2359300
  523.4 6.3 %copy-start.45 = (f32[768,256]{1,0:T(8,128)S(1)}, f32[768,256]{1,0:T(8,128)}, u32[]{:S(2)}) copy-start(f32[768,256]{1,0:T(8,128)} %get-tuple-element.57) | copy-start | bytes 2359300
  553.1 3.6 copy-start.60
  558.7 3.8 slice-start
  558.7 3.9 slice-start.1
  558.7 4.3 copy-start.4
  558.7 4.3 copy-start.22
  558.7 4.4 copy-start.28
  563.9 1.1 copy-start.7
  563.9 1.4 copy-start.13
  563.9 1.6 copy-start.14
  563.9 1.6 copy-start.40
  564.0 1.7 copy-start.41
  564.0 1.7 copy-start.52
  564.0 1.7 copy-start.54
  564.0 1.7 copy-start.56
  564.0 1.7 copy-start.58
  (4 other events, 3.1 us)
Sparse Core Ops, SparseCore 0:
  43.8 131.7 all-reduce.11
  178.0 59.1 all-reduce.13
  239.3 63.0 all-gather.2
  325.1 136.4 all-reduce.15
  463.8 86.1 all-reduce.17
